TPU v7x, 32 devices: a whole 2x2x4 slice. The times are simulated.
32 devices in a mesh: sector: 8 (over y, x, core), term: 4 (over z).
Axes of the slice: x: 2, y: 2, z: 4, core: 2. Of those that a mesh axis runs over, the one named last changes fastest.
Arguments:
- wave: float32 [8, 512, 512], P('sector', 'term'), may hold values from -12 to 12
- left_ops: bfloat16 [16, 8, 512, 512], P('term', 'sector'), may hold values from -4 to 4
- right_ops: bfloat16 [16, 8, 512, 512], P('term', 'sector'), may hold values from -4 to 4
- charges: int32 [16], replicated, may hold values from -1 to 1, as said below
- diag: float32 [8, 512, 512], P('sector', 'term'), may hold values from 0.5 to 8
Outputs:
- psi_out: float32 [8, 512, 512], P('sector', 'term')
Inputs may be any that keep to these rules, and one draw needn't show every extreme that they name: `charges`: exactly (17) // 2 terms have charge 0; at least one term has charge 1 and at least one has charge -1.
All inputs are finite; a program needn't handle non-finite values.
Results may differ from a plain program's by a relative error of at most 0.0085.
Values may be sent and summed in bfloat16 or wider, within the bound.
No kernel may reach another device: no remote copies, remote signals or barrier semaphores. Data moves between devices by JAX's collectives and lax.ppermute only.
A program may use at most 64 MiB of HBM per device.

v0:
```python
import jax
import jax.numpy as jnp
from jax import lax
from jax.sharding import PartitionSpec as P

STEPS = 3


def from_behind(value, axis, steps):
    count = lax.axis_size(axis)
    leading, last = (max(0, -steps), min(count, count - steps))
    return lax.ppermute(value, axis, [(source, source + steps) for source in range(leading, last)])


def apply_terms(left_ops, right_ops, my_charges, own, lower, upper):
    stacked = jnp.stack([upper, own, lower])
    picked = stacked[my_charges + 1]
    inner = jnp.einsum(
        "tij,tjk->tik", left_ops[:, 0], picked, preferred_element_type=jnp.float32
    ).astype(jnp.bfloat16)
    image = jnp.einsum("tij,tkj->tik", inner, right_ops[:, 0], preferred_element_type=jnp.float32)
    return jnp.sum(image, axis=0)


def per_device(wave, left_ops, right_ops, charges, diag):
    per_dev = left_ops.shape[0]
    my_charges = lax.dynamic_slice_in_dim(charges, lax.axis_index("term") * per_dev, per_dev)
    psi, full_diag = (
        lax.all_gather(wave[0], "term", axis=0, tiled=True),
        lax.all_gather(diag[0], "term", axis=0, tiled=True),
    )
    for step in range(STEPS):
        wb = psi.astype(jnp.bfloat16)
        lower = from_behind(wb, "sector", 1)
        upper = from_behind(wb, "sector", -1)
        partial_image = apply_terms(left_ops, right_ops, my_charges, wb, lower, upper)
        hpsi = lax.psum(partial_image, "term")
        cross, square = lax.psum((jnp.sum(psi * hpsi), jnp.sum(psi * psi)), "sector")
        theta = cross / square
        fresh = psi - (hpsi - theta * psi) / jnp.maximum(jnp.abs(full_diag - theta), 1.0)
        total = lax.psum(jnp.sum(fresh * fresh), "sector")
        psi = fresh / jnp.sqrt(total / (lax.axis_size("sector") * fresh.size) + 1e-06)
    rows_dev = wave.shape[1]
    result = lax.dynamic_slice_in_dim(psi, lax.axis_index("term") * rows_dev, rows_dev, 0)
    return result[None]


def solution(mesh):
    in_specs = (
        P("sector", "term", None),
        P("term", "sector", None, None),
        P("term", "sector", None, None),
        P(),
        P("sector", "term", None),
    )
    out_specs = P("sector", "term", None)
    return jax.shard_map(
        per_device, mesh=mesh, in_specs=in_specs, out_specs=out_specs, check_vma=False
    )
```

profile of v0, /device:TPU:0, one launch (start us, length us, event | category | flops | bytes accessed | tf_op | source)
XLA Modules:
  0.0 397.1 jit_solution(17423861717904664301)
XLA Ops:
  7.3 32.3 %all-gather.5.cloned.1.call-done = f32[1,512,512]{2,1,0:T(8,128)} async-done(((f32[1,128,512]{2,1,0:T(8,128)}), f32[1,512,512]{2,1,0:T(8,128)}) %all-gather.5.cloned.1.call-update) | async-done | bytes 1048592 | tf_op jit(solution)/shard_map/all_gather | solution.py:29
  46.0 2.9 collective-permute-done
  49.0 2.5 pad_maximum_fusion
  51.5 3.4 gather_fusion
  54.9 5.5 %fusion.30 = f32[512,512]{1,0:T(8,128)} fusion(bf16[4,1,512,512]{3,2,1,0:T(8,128)(2,1)S(1)} %copy-done, bf16[4,512,512]{2,1,0:T(8,128)(2,1)} %gather_fusion, bf16[4,1,512,512]{3,2,1,0:T(8,128)(2,1)} %param.6), kind=kOutput, calls=%fused_computation.24 | convolution fusion | flops 2148532224 | bytes 7340032 | tf_op jit(solution)/shard_map/tij,tkj->tik/dot_general | solution.py:21
  61.3 59.4 %all-reduce.7.cloned.1.call-done = f32[512,512]{1,0:T(8,128)} async-done(((f32[512,512]{1,0:T(8,128)}), f32[512,512]{1,0:T(8,128)}) %all-reduce.7.cloned.1.call-update) | async-done | bytes 1048592 | tf_op jit(solution)/shard_map/psum | solution.py:37
  122.8 14.7 %all-reduce.2 = (f32[]{:T(128)}, f32[]{:T(128)}) all-reduce(f32[]{:T(128)} %get-tuple-element.10, f32[]{:T(128)} %get-tuple-element.9), channel_id=1, replica_groups=mesh['sector'=8,'term'=4] {'sector'}, use_global_device_ids=true, to_apply=%region_2.0 | all-reduce | flops 2 | bytes 16 | tf_op jit(solution)/shard_map/psum | solution.py:38
  138.8 10.7 %all-gather.7.cloned.1.call-done = f32[1,512,512]{2,1,0:T(8,128)} async-done(((f32[1,128,512]{2,1,0:T(8,128)}), f32[1,512,512]{2,1,0:T(8,128)}) %all-gather.7.cloned.1.call-update) | async-done | bytes 1048592 | tf_op jit(solution)/shard_map/all_gather | solution.py:30
  149.5 2.8 multiply_reduce_fusion.6
  152.4 13.7 %psum.87 = f32[]{:T(128)} all-reduce(f32[]{:T(128)} %get-tuple-element.21), channel_id=1, replica_groups=mesh['sector'=8,'term'=4] {'sector'}, use_global_device_ids=true, to_apply=%region_6.0 | all-reduce | flops 1 | bytes 8 | tf_op jit(solution)/shard_map/psum | solution.py:41
  169.7 2.3 collective-permute-done.2
  173.4 3.4 gather_fusion.1
  176.8 5.5 %fusion.37 = f32[512,512]{1,0:T(8,128)} fusion(bf16[4,1,512,512]{3,2,1,0:T(8,128)(2,1)S(1)} %copy-done, bf16[4,512,512]{2,1,0:T(8,128)(2,1)} %gather_fusion.1, bf16[4,1,512,512]{3,2,1,0:T(8,128)(2,1)} %param.6), kind=kOutput, calls=%fused_computation.25 | convolution fusion | flops 2148532224 | bytes 7340032 | tf_op jit(solution)/shard_map/tij,tkj->tik/dot_general | solution.py:21
  182.4 60.9 %all-reduce.9.cloned.1.call-done = f32[512,512]{1,0:T(8,128)} async-done(((f32[512,512]{1,0:T(8,128)}), f32[512,512]{1,0:T(8,128)}) %all-reduce.9.cloned.1.call-update) | async-done | bytes 1048592 | tf_op jit(solution)/shard_map/psum | solution.py:37
  245.5 14.3 %all-reduce.1 = (f32[]{:T(128)}, f32[]{:T(128)}) all-reduce(f32[]{:T(128)} %get-tuple-element.8, f32[]{:T(128)} %get-tuple-element.7), channel_id=1, replica_groups=mesh['sector'=8,'term'=4] {'sector'}, use_global_device_ids=true, to_apply=%region_9.0 | all-reduce | flops 2 | bytes 16 | tf_op jit(solution)/shard_map/psum | solution.py:38
  261.1 3.6 multiply_reduce_fusion.3
  264.6 12.4 %psum.91 = f32[]{:T(128)} all-reduce(f32[]{:T(128)} %get-tuple-element.19), channel_id=1, replica_groups=mesh['sector'=8,'term'=4] {'sector'}, use_global_device_ids=true, to_apply=%region_13.0 | all-reduce | flops 1 | bytes 8 | tf_op jit(solution)/shard_map/psum | solution.py:41
  282.4 2.3 collective-permute-done.4
  286.0 3.4 gather_fusion.2
  289.5 5.5 %fusion.44 = f32[512,512]{1,0:T(8,128)} fusion(bf16[4,1,512,512]{3,2,1,0:T(8,128)(2,1)S(1)} %copy-done, bf16[4,512,512]{2,1,0:T(8,128)(2,1)} %gather_fusion.2, bf16[4,1,512,512]{3,2,1,0:T(8,128)(2,1)} %param.6), kind=kOutput, calls=%fused_computation.26 | convolution fusion | flops 2148532224 | bytes 7340032 | tf_op jit(solution)/shard_map/tij,tkj->tik/dot_general | solution.py:21
  295.0 59.5 %all-reduce.11.cloned.1.call-done = f32[512,512]{1,0:T(8,128)} async-done(((f32[512,512]{1,0:T(8,128)}), f32[512,512]{1,0:T(8,128)}) %all-reduce.11.cloned.1.call-update) | async-done | bytes 1048592 | tf_op jit(solution)/shard_map/psum | solution.py:37
  356.7 14.3 %all-reduce = (f32[]{:T(128)}, f32[]{:T(128)}) all-reduce(f32[]{:T(128)} %get-tuple-element.6, f32[]{:T(128)} %get-tuple-element.5), channel_id=1, replica_groups=mesh['sector'=8,'term'=4] {'sector'}, use_global_device_ids=true, to_apply=%region_16.0 | all-reduce | flops 2 | bytes 16 | tf_op jit(solution)/shard_map/psum | solution.py:38
  372.3 3.6 multiply_reduce_fusion
  375.8 12.4 %psum.95 = f32[]{:T(128)} all-reduce(f32[]{:T(128)} %get-tuple-element.17), channel_id=1, replica_groups=mesh['sector'=8,'term'=4] {'sector'}, use_global_device_ids=true, to_apply=%region_20.0 | all-reduce | flops 1 | bytes 8 | tf_op jit(solution)/shard_map/psum | solution.py:41
  (39 shorter events, 26.4 us)
Async XLA Ops:
  6.5 48.4 %copy-start = (bf16[4,1,512,512]{3,2,1,0:T(8,128)(2,1)S(1)}, bf16[4,1,512,512]{3,2,1,0:T(8,128)(2,1)}, u32[]{:S(2)}) copy-start(bf16[4,1,512,512]{3,2,1,0:T(8,128)(2,1)} %param.7) | copy-start | bytes 6291460
  6.5 33.1 %all-gather.5.cloned.1.call-start = ((), (), s32[]{:S(2)}) async-start(), calls=%async_computation.3 | async-start | bytes 1310720 | tf_op jit(solution)/shard_map/all_gather | solution.py:29
  7.3 113.4 %all-reduce.7.cloned.1.call-start = ((), (), s32[]{:S(2)}) async-start(), calls=%async_computation | async-start | bytes 2097152 | tf_op jit(solution)/shard_map/psum | solution.py:37
  39.6 6.3 %copy-start.2 = (f32[1,512,512]{2,1,0:T(8,128)S(1)}, f32[1,512,512]{2,1,0:T(8,128)}, u32[]{:S(2)}) copy-start(f32[1,512,512]{2,1,0:T(8,128)} %all-gather.5.cloned.1.call-done) | copy-start | bytes 3145732
  41.8 4.2 %collective-permute-start.1 = (bf16[512,512]{1,0:T(8,128)(2,1)}, bf16[512,512]{1,0:T(8,128)(2,1)}, u32[]{:S(2)}, u32[]{:S(2)}) collective-permute-start(bf16[512,512]{1,0:T(8,128)(2,1)} %bitcast_convert_fusion), channel_id=1, source_target_pairs={{0,4},{4,8},{8,12},{12,16},{16,20},{20,24},{24,28},{1,5},{5,9},{9,... | collective-permute-start | bytes 1572872 | tf_op jit(solution)/shard_map/ppermute | solution.py:12
  43.9 5.0 %collective-permute-start = (bf16[512,512]{1,0:T(8,128)(2,1)}, bf16[512,512]{1,0:T(8,128)(2,1)}, u32[]{:S(2)}, u32[]{:S(2)}) collective-permute-start(bf16[512,512]{1,0:T(8,128)(2,1)} %bitcast_convert_fusion), channel_id=1, source_target_pairs={{4,0},{8,4},{12,8},{16,12},{20,16},{24,20},{28,24},{5,1},{9,5},{13... | collective-permute-start | bytes 1572872 | tf_op jit(solution)/shard_map/ppermute | solution.py:12
  60.5 89.0 %all-gather.7.cloned.1.call-start = ((), (), s32[]{:S(2)}) async-start(), calls=%async_computation.4 | async-start | bytes 1310720 | tf_op jit(solution)/shard_map/all_gather | solution.py:30
  61.2 182.1 %all-reduce.9.cloned.1.call-start = ((), (), s32[]{:S(2)}) async-start(), calls=%async_computation.1 | async-start | bytes 2097152 | tf_op jit(solution)/shard_map/psum | solution.py:37
  166.9 2.8 collective-permute-start.3
  168.2 3.8 collective-permute-start.2
  182.4 172.1 %all-reduce.11.cloned.1.call-start = ((), (), s32[]{:S(2)}) async-start(), calls=%async_computation.2 | async-start | bytes 2097152 | tf_op jit(solution)/shard_map/psum | solution.py:37
  264.6 17.6 %copy-start.1 = (f32[512,512]{1,0:T(8,128)S(1)}, f32[512,512]{1,0:T(8,128)}, u32[]{:S(2)}) copy-start(f32[512,512]{1,0:T(8,128)} %get-tuple-element.20) | copy-start | bytes 3145732
  279.1 3.3 collective-permute-start.5
  280.9 3.8 collective-permute-start.4
Sparse Core Ops, SparseCore 0:
  8.9 30.6 all-gather.4
  60.6 59.9 all-reduce.6
  122.2 27.2 all-gather.6
  182.5 60.7 all-reduce.8
  295.2 59.3 all-reduce.10
where the time goes:
time: 398 us; the launch traced here: 397 us
  waiting for transfers between devices  232 us (58%)
  blocking collectives  81.9 us (21%)
  other arithmetic  28 us (7%)
  between operations  19.1 us (5%)
  matrix products  16.6 us (4%)
  local copies, waits for them, and re-layouts  10.3 us (3%)
  starting transfers between devices  9.25 us (2%)
    psum x3, waiting for transfers between devices, per_device(): hpsi = lax.psum(partial_image, 'term')  180 us
    psum x3, blocking collectives, per_device(): lax.psum((jnp.sum(psi * hpsi), jnp.sum(psi * psi)), 'sector')  43.4 us
    psum x3, blocking collectives, per_device(): total = lax.psum(jnp.sum(fresh * fresh), 'sector')  38.6 us
    all_gather x1, waiting for transfers between devices, per_device(): lax.all_gather(wave[0], 'term', axis=0, tiled=True)  32.3 us
    dot_general x3, matrix products, apply_terms(): jnp.einsum('tij,tkj->tik', inner, right_ops[:, 0], preferred_element_type...  16.6 us
    all_gather x1, waiting for transfers between devices, per_device(): lax.all_gather(diag[0], 'term', axis=0, tiled=True)  10.7 us
    gather x3, local copies, waits for them, and re-layouts, apply_terms(): picked = stacked[my_charges + 1]  10.3 us
    reduce_sum x3, other arithmetic, per_device(): total = lax.psum(jnp.sum(fresh * fresh), 'sector')  9.95 us
  transfers between devices with their start and end apart: 11, of which 10 were waited for; matrix products, arithmetic and copies ran while one was open for 1% of the time, Pallas kernels for 0%

commit v1 on v0

v1 whole, which is shorter than its diff:
```python
import functools

import jax
import jax.numpy as jnp
from jax import lax
from jax.experimental import pallas as pl
from jax.experimental.pallas import tpu as pltpu
from jax.sharding import PartitionSpec as P

STEPS = 3
F32, BF16 = jnp.float32, jnp.bfloat16
NT = (((1,), (1,)), ((), ()))
VMEM = pl.BlockSpec(memory_space=pltpu.VMEM)
SMEM = pl.BlockSpec(memory_space=pltpu.SMEM)
PARAMS = pltpu.CompilerParams(vmem_limit_bytes=40 << 20)


def exchange(value, k):
    count = lax.axis_size("term")
    return lax.ppermute(value, "term", [(i, i ^ k) for i in range(count)])


def swap_near(value):
    count = lax.axis_size("sector")
    return lax.ppermute(value, "sector", [(i, i ^ 1) for i in range(count)])


def swap_far(value):
    count = lax.axis_size("sector")
    return lax.ppermute(
        value, "sector", [(i, (i + 1 if i % 2 else i - 1) % count) for i in range(count)]
    )


def lane_sums(*values):
    lane = lax.broadcasted_iota(jnp.int32, (1, 128), 1)
    row = jnp.zeros((1, 128), F32)
    for i, value in enumerate(values):
        row = jnp.where(lane == i, value, row)
    return row


def total(v):
    return jnp.sum(jnp.sum(v, axis=1, keepdims=True), axis=0, keepdims=True)


def matmul_kernel(groups, sel, left, right, *refs):
    n_own = groups
    own = refs[:n_own]
    near, far_a, far_b, stats = refs[n_own : n_own + 4]
    mine = refs[n_own + 4]
    away = refs[n_own + 5 : 2 * n_own + 4]
    row = refs[2 * n_own + 4]
    src, acc = refs[2 * n_own + 5 :]
    terms, size = left.shape[0], left.shape[1]
    rows = size // groups
    place = sel[terms + 2]
    half = far_a.shape[0]
    for k in range(groups):
        at = pl.ds(pl.multiple_of((place ^ k) * rows, rows), rows)
        src[1, at] = own[k][...]
        src[sel[terms], at] = near[k]
        src[sel[terms + 1], at] = far_a[k] if k < half else far_b[k - half]
    src[3] = jnp.zeros((size, size), BF16)
    for t in range(terms):
        inner = jnp.dot(left[t], src[sel[t]], preferred_element_type=F32).astype(BF16)
        image = lax.dot_general(inner, right[t], NT, preferred_element_type=F32)
        if t == 0:
            acc[...] = image
        else:
            acc[...] += image
    cross = total(acc[...] * src[1].astype(F32))
    row[...] = stats[...] + lane_sums(cross)
    for k in range(groups):
        at = pl.ds(pl.multiple_of((place ^ k) * rows, rows), rows)
        if k == 0:
            mine[...] = acc[at]
        else:
            away[k - 1][...] = acc[at].astype(BF16)


def apply_terms(sel, left, right, own, near, far_a, far_b, stats):
    groups = len(own)
    rows, size = own[0].shape
    return pl.pallas_call(
        functools.partial(matmul_kernel, groups),
        out_shape=[jax.ShapeDtypeStruct((rows, size), F32)]
        + [jax.ShapeDtypeStruct((rows, size), BF16)] * (groups - 1)
        + [jax.ShapeDtypeStruct((1, 128), F32)],
        in_specs=[SMEM] + [VMEM] * (groups + 6),
        out_specs=[VMEM] * (groups + 1),
        scratch_shapes=[pltpu.VMEM((4, size, size), BF16), pltpu.VMEM((size, size), F32)],
        compiler_params=PARAMS,
        name="apply_terms",
    )(sel, left, right, *own, near, far_a, far_b, stats)


def update_kernel(count, n_away, first, sums, fresh, diag, mine, *refs):
    away = refs[:n_away]
    new, rounded, stats = refs[n_away:]
    image = mine[...]
    for ref in away:
        image = image + ref[...].astype(F32)
    table = jnp.sum(sums[...], axis=0)
    theta = table[:, 0:1] / table[:, 1:2]
    old = fresh[...]
    value = old - (image - theta * old) / jnp.maximum(jnp.abs(diag[...] - theta), 1.0)
    if not first:
        value = value / jnp.sqrt(table[:, 2:3] / count + 1e-06)
    new[...] = value
    low = value.astype(BF16)
    rounded[...] = low
    stats[...] = lane_sums(0.0, total(low.astype(F32) * value), total(value * value))


def update(count, first, sums, fresh, diag, mine, away):
    shape = fresh.shape
    return pl.pallas_call(
        functools.partial(update_kernel, count, len(away), first),
        out_shape=[
            jax.ShapeDtypeStruct(shape, F32),
            jax.ShapeDtypeStruct(shape, BF16),
            jax.ShapeDtypeStruct((1, 128), F32),
        ],
        in_specs=[VMEM] * (4 + len(away)),
        out_specs=[VMEM] * 3,
        compiler_params=PARAMS,
        name="update",
    )(sums, fresh, diag, mine, *away)


def everyone(row):
    axes = ("sector", "term")
    count = lax.axis_size(axes)
    return lax.all_to_all(jnp.broadcast_to(row[None], (count, 1, 128)), axes, 0, 0)


def per_device(wave, left_ops, right_ops, charges, diag):
    terms = left_ops.shape[0]
    left, right = left_ops[:, 0], right_ops[:, 0]
    groups, sectors = lax.axis_size("term"), lax.axis_size("sector")
    place, sector = lax.axis_index("term"), lax.axis_index("sector")
    moved = lax.dynamic_slice_in_dim(charges, place * terms, terms)
    inside = (sector - moved >= 0) & (sector - moved < sectors)
    source = jnp.where(inside, moved + 1, 3)
    odd = sector % 2
    sel = jnp.concatenate([source, jnp.stack([2 * odd, 2 - 2 * odd, place])]).astype(jnp.int32)

    fresh, rows = wave[0], diag[0]
    count = fresh.size * groups * sectors
    rounded = fresh.astype(BF16)
    stats = lane_sums(0.0, jnp.sum(rounded.astype(F32) * fresh), jnp.sum(fresh * fresh))
    for step in range(STEPS):
        own = [rounded] + [exchange(rounded, k) for k in range(1, groups)]
        half = groups // 2
        far_a = swap_far(jnp.stack(own[:half]))
        far_b = swap_far(jnp.stack(own[half:]))
        near = swap_near(jnp.stack(own))
        mine, *rest = apply_terms(sel, left, right, own, near, far_a, far_b, stats)
        away, row = rest[:-1], rest[-1]
        got = [exchange(away[k - 1], k) for k in range(groups - 1, 0, -1)]
        sums = everyone(row)
        fresh, rounded, stats = update(count, step == 0, sums, fresh, rows, mine, got)
    sums = everyone(stats)
    norm = jnp.sum(sums, axis=0)[0, 2]
    return (fresh / jnp.sqrt(norm / count + 1e-06))[None]


def solution(mesh):
    in_specs = (
        P("sector", "term", None),
        P("term", "sector", None, None),
        P("term", "sector", None, None),
        P(),
        P("sector", "term", None),
    )
    out_specs = P("sector", "term", None)
    return jax.shard_map(
        per_device, mesh=mesh, in_specs=in_specs, out_specs=out_specs, check_vma=False
    )
```

time: 398 us -> 160 us (0.40)
  waiting for transfers between devices: 232 us -> 61.9 us
  blocking collectives: 81.9 us -> 39.1 us
  starting transfers between devices: 9.25 us -> 36.2 us
  other arithmetic: 28 us -> 7.68 us
  between operations: 19.1 us -> 0.85 us
  matrix products: 16.6 us -> 0 us
  Pallas kernels: 0 us -> 11.7 us
  local copies, waits for them, and re-layouts: 10.3 us -> 2.23 us
    psum x3 -> x0, waiting for transfers between devices: 180 us -> none  [per_device(): hpsi = lax.psum(partial_image, 'term')]
    psum x6 -> x0, blocking collectives: 81.9 us -> none  [the longest x3 43.4 us: per_device(): lax.psum((jnp.sum(psi * hpsi), jnp.sum(psi * psi)), 'sector')]
    ppermute x6 -> x27, waiting for transfers between devices: 7.66 us -> 61.9 us  [the longest x6 34.6 us: swap_far(): lax.ppermute(value, 'sector', [(i, (i + 1 if i % 2 else i - 1) % count) f...]
    all_gather x2 -> x0, waiting for transfers between devices: 43 us -> none  [the longest x1 32.3 us: per_device(): lax.all_gather(wave[0], 'term', axis=0, tiled=True)]
    all_to_all x0 -> x4, blocking collectives: none -> 39.1 us  [everyone(): lax.all_to_all(jnp.broadcast_to(row[None], (count, 1, 128)), axes, 0, 0)]
    ppermute x6 -> x27, starting transfers between devices: 9.09 us -> 36.2 us  [the longest x18 28 us: exchange(): return lax.ppermute(value, 'term', [(i, i ^ k) for i in range(count)])]
    dot_general x3 -> x0, matrix products: 16.6 us -> none  [apply_terms(): jnp.einsum('tij,tkj->tik', inner, right_ops[:, 0], preferred_element_type...]
    reduce_sum x6 -> x2, other arithmetic: 16.5 us -> 1.71 us  [the longest x1 1.69 us: per_device(): jnp.sum(fresh * fresh)]
  transfers between devices with their start and end apart: 11 -> 27, of which waited for: 10 -> 12; matrix products, arithmetic and copies ran while one was open for 1% -> 3% of each run, Pallas kernels for 0% -> 0%
where the time goes in v1:
time: 160 us
  waiting for transfers between devices  61.9 us (39%)
  blocking collectives  39.1 us (24%)
  starting transfers between devices  36.2 us (23%)
  Pallas kernels  11.7 us (7%)
  other arithmetic  7.68 us (5%)
  local copies, waits for them, and re-layouts  2.23 us (1%)
    all_to_all x4, blocking collectives, everyone(): lax.all_to_all(jnp.broadcast_to(row[None], (count, 1, 128)), axes, 0, 0)  39.1 us
    ppermute x6, waiting for transfers between devices, swap_far(): lax.ppermute(value, 'sector', [(i, (i + 1 if i % 2 else i - 1) % count) f...  34.6 us
    ppermute x18, starting transfers between devices, exchange(): return lax.ppermute(value, 'term', [(i, i ^ k) for i in range(count)])  28 us
    ppermute x18, waiting for transfers between devices, exchange(): return lax.ppermute(value, 'term', [(i, i ^ k) for i in range(count)])  27.3 us
    pallas_call x3, Pallas kernels, apply_terms(): pl.pallas_call(functools.partial(matmul_kernel, groups), out_shape=[jax.S...  9.98 us
    ppermute x6, starting transfers between devices, swap_far(): lax.ppermute(value, 'sector', [(i, (i + 1 if i % 2 else i - 1) % count) f...  8.06 us
  transfers between devices with their start and end apart: 27, of which 12 were waited for; matrix products, arithmetic and copies ran while one was open for 3% of the time, Pallas kernels for 0%

profile of v1, /device:TPU:0, one launch (start us, length us, event | category | flops | bytes accessed | tf_op | source)
XLA Modules:
  0.0 159.6 jit_solution(11316319808828074679)
XLA Ops:
  1.2 5.1 %collective-permute-start.2 = (bf16[128,512]{1,0:T(8,128)(2,1)S(1)}, bf16[128,512]{1,0:T(8,128)(2,1)S(1)}, u32[]{:S(2)}, u32[]{:S(2)}) collective-permute-start(bf16[128,512]{1,0:T(8,128)(2,1)S(1)} %get-tuple-element.54.refs_0_), channel_id=1, source_target_pairs={{0,3},{1,2},{2,1},{3,0},{4,7},{5,6},{6,5},{7,4},{8,11},{9,10},{10,... | collective-permute-start | bytes 393224 | tf_op jit(solution)/shard_map/ppermute | solution.py:20
  10.8 6.6 %collective-permute-done.1.refs_2_ = bf16[128,512]{1,0:T(8,128)(2,1)S(1)} collective-permute-done((bf16[128,512]{1,0:T(8,128)(2,1)S(1)}, bf16[128,512]{1,0:T(8,128)(2,1)S(1)}, u32[]{:S(2)}, u32[]{:S(2)}) %collective-permute-start.1) | collective-permute-done | bytes 131104 | tf_op jit(solution)/shard_map/ppermute | solution.py:20
  19.1 2.6 %collective-permute-start.5 = (bf16[2,128,512]{2,1,0:T(8,128)(2,1)}, bf16[2,128,512]{2,1,0:T(8,128)(2,1)S(1)}, u32[]{:S(2)}, u32[]{:S(2)}) collective-permute-start(bf16[2,128,512]{2,1,0:T(8,128)(2,1)} %pad_maximum_fusion.4), channel_id=1, source_target_pairs={{0,28},{4,8},{8,4},{12,16},{16,12},{20,24},{24,20},{28,0},{1,29},{... | collective-permute-start | bytes 786440 | tf_op jit(solution)/shard_map/ppermute | solution.py:30
  23.9 4.8 %collective-permute-done.5.refs_6_ = bf16[2,128,512]{2,1,0:T(8,128)(2,1)S(1)} collective-permute-done((bf16[2,128,512]{2,1,0:T(8,128)(2,1)}, bf16[2,128,512]{2,1,0:T(8,128)(2,1)S(1)}, u32[]{:S(2)}, u32[]{:S(2)}) %collective-permute-start.5) | collective-permute-done | bytes 262176 | tf_op jit(solution)/shard_map/ppermute | solution.py:30
  28.6 5.1 %collective-permute-done.4.refs_5_ = bf16[2,128,512]{2,1,0:T(8,128)(2,1)} collective-permute-done((bf16[2,128,512]{2,1,0:T(8,128)(2,1)}, bf16[2,128,512]{2,1,0:T(8,128)(2,1)}, u32[]{:S(2)}, u32[]{:S(2)}) %collective-permute-start.4) | collective-permute-done | bytes 262176 | tf_op jit(solution)/shard_map/ppermute | solution.py:30
  35.4 3.6 %apply_terms.3 = (f32[128,512]{1,0:T(8,128)S(1)}, bf16[128,512]{1,0:T(8,128)(2,1)S(1)}, bf16[128,512]{1,0:T(8,128)(2,1)S(1)}, bf16[128,512]{1,0:T(8,128)(2,1)S(1)}, f32[1,128]{1,0:T(1,128)S(1)}) custom-call(s32[7]{0:T(128)S(1)} %pad_add_fusion.sel, bf16[4,512,512]{2,1,0:T(8,128)(2,1)S(1)} %bitcast.32, bf16[4,512,512]{2,1,0:T(8,128)(2,1)S(1)} %bitcast.35, ...), custom_call_target="tpu_custom_call" | custom-call | tf_op jit(solution)/shard_map/apply_terms/pallas_call | solution.py:85
  39.0 2.5 %collective-permute-start.6 = (bf16[128,512]{1,0:T(8,128)(2,1)S(1)}, bf16[128,512]{1,0:T(8,128)(2,1)S(1)}, u32[]{:S(2)}, u32[]{:S(2)}) collective-permute-start(bf16[128,512]{1,0:T(8,128)(2,1)S(1)} %get-tuple-element.30), channel_id=1, source_target_pairs={{0,3},{1,2},{2,1},{3,0},{4,7},{5,6},{6,5},{7,4},{8,11},{9,10},{10,... | collective-permute-start | bytes 393224 | tf_op jit(solution)/shard_map/ppermute | solution.py:20
  43.5 11.3 %all_to_all.20.sums = f32[32,1,128]{2,1,0:T(1,128)S(1)} all-to-all(f32[32,1,128]{2,1,0:T(1,128)S(1)} %broadcast_in_dim.56), channel_id=1, replica_groups=mesh['sector'=8,'term'=4] {'sector','term'}, dimensions={0} | all-to-all | bytes 32768 | tf_op jit(solution)/shard_map/all_to_all | solution.py:135
  57.2 2.4 %collective-permute-start.9 = (bf16[128,512]{1,0:T(8,128)(2,1)S(1)}, bf16[128,512]{1,0:T(8,128)(2,1)S(1)}, u32[]{:S(2)}, u32[]{:S(2)}) collective-permute-start(bf16[128,512]{1,0:T(8,128)(2,1)S(1)} %get-tuple-element.33.refs_0_), channel_id=1, source_target_pairs={{0,1},{1,0},{2,3},{3,2},{4,5},{5,4},{6,7},{7,6},{8,9},{9,8},{10,11... | collective-permute-start | bytes 393224 | tf_op jit(solution)/shard_map/ppermute | solution.py:20
  59.6 3.8 %collective-permute-done.11.refs_3_ = bf16[128,512]{1,0:T(8,128)(2,1)S(1)} collective-permute-done((bf16[128,512]{1,0:T(8,128)(2,1)S(1)}, bf16[128,512]{1,0:T(8,128)(2,1)S(1)}, u32[]{:S(2)}, u32[]{:S(2)}) %collective-permute-start.11) | collective-permute-done | bytes 131104 | tf_op jit(solution)/shard_map/ppermute | solution.py:20
  63.4 5.4 %collective-permute-done.10.refs_2_ = bf16[128,512]{1,0:T(8,128)(2,1)S(1)} collective-permute-done((bf16[128,512]{1,0:T(8,128)(2,1)S(1)}, bf16[128,512]{1,0:T(8,128)(2,1)S(1)}, u32[]{:S(2)}, u32[]{:S(2)}) %collective-permute-start.10) | collective-permute-done | bytes 131104 | tf_op jit(solution)/shard_map/ppermute | solution.py:20
  71.8 6.9 %collective-permute-done.14.refs_6_ = bf16[2,128,512]{2,1,0:T(8,128)(2,1)S(1)} collective-permute-done((bf16[2,128,512]{2,1,0:T(8,128)(2,1)S(1)}, bf16[2,128,512]{2,1,0:T(8,128)(2,1)S(1)}, u32[]{:S(2)}, u32[]{:S(2)}) %collective-permute-start.14) | collective-permute-done | bytes 262176 | tf_op jit(solution)/shard_map/ppermute | solution.py:30
  78.7 5.4 %collective-permute-done.13.refs_5_ = bf16[2,128,512]{2,1,0:T(8,128)(2,1)S(1)} collective-permute-done((bf16[2,128,512]{2,1,0:T(8,128)(2,1)S(1)}, bf16[2,128,512]{2,1,0:T(8,128)(2,1)S(1)}, u32[]{:S(2)}, u32[]{:S(2)}) %collective-permute-start.13) | collective-permute-done | bytes 262176 | tf_op jit(solution)/shard_map/ppermute | solution.py:30
  84.1 3.2 %apply_terms.4 = (f32[128,512]{1,0:T(8,128)S(1)}, bf16[128,512]{1,0:T(8,128)(2,1)S(1)}, bf16[128,512]{1,0:T(8,128)(2,1)S(1)}, bf16[128,512]{1,0:T(8,128)(2,1)S(1)}, f32[1,128]{1,0:T(1,128)S(1)}) custom-call(s32[7]{0:T(128)S(1)} %pad_add_fusion.sel, bf16[4,512,512]{2,1,0:T(8,128)(2,1)S(1)} %bitcast.33, bf16[4,512,512]{2,1,0:T(8,128)(2,1)S(1)} %bitcast.36, ...), custom_call_target="tpu_custom_call" | custom-call | tf_op jit(solution)/shard_map/apply_terms/pallas_call | solution.py:85
  88.7 2.9 %collective-permute-start.17 = (bf16[128,512]{1,0:T(8,128)(2,1)S(1)}, bf16[128,512]{1,0:T(8,128)(2,1)S(1)}, u32[]{:S(2)}, u32[]{:S(2)}) collective-permute-start(bf16[128,512]{1,0:T(8,128)(2,1)S(1)} %get-tuple-element.40), channel_id=1, source_target_pairs={{0,1},{1,0},{2,3},{3,2},{4,5},{5,4},{6,7},{7,6},{8,9},{9,8},{10,11... | collective-permute-start | bytes 393224 | tf_op jit(solution)/shard_map/ppermute | solution.py:20
  91.7 8.9 %all_to_all.21.sums = f32[32,1,128]{2,1,0:T(1,128)S(1)} all-to-all(f32[32,1,128]{2,1,0:T(1,128)S(1)} %broadcast_in_dim.58), channel_id=1, replica_groups=mesh['sector'=8,'term'=4] {'sector','term'}, dimensions={0} | all-to-all | bytes 32768 | tf_op jit(solution)/shard_map/all_to_all | solution.py:135
  105.4 3.8 %collective-permute-done.20.refs_3_ = bf16[128,512]{1,0:T(8,128)(2,1)S(1)} collective-permute-done((bf16[128,512]{1,0:T(8,128)(2,1)S(1)}, bf16[128,512]{1,0:T(8,128)(2,1)S(1)}, u32[]{:S(2)}, u32[]{:S(2)}) %collective-permute-start.20) | collective-permute-done | bytes 131104 | tf_op jit(solution)/shard_map/ppermute | solution.py:20
  109.3 5.4 %collective-permute-done.19.refs_2_ = bf16[128,512]{1,0:T(8,128)(2,1)S(1)} collective-permute-done((bf16[128,512]{1,0:T(8,128)(2,1)S(1)}, bf16[128,512]{1,0:T(8,128)(2,1)S(1)}, u32[]{:S(2)}, u32[]{:S(2)}) %collective-permute-start.19) | collective-permute-done | bytes 131104 | tf_op jit(solution)/shard_map/ppermute | solution.py:20
  117.6 6.9 %collective-permute-done.23.refs_6_ = bf16[2,128,512]{2,1,0:T(8,128)(2,1)S(1)} collective-permute-done((bf16[2,128,512]{2,1,0:T(8,128)(2,1)S(1)}, bf16[2,128,512]{2,1,0:T(8,128)(2,1)S(1)}, u32[]{:S(2)}, u32[]{:S(2)}) %collective-permute-start.23) | collective-permute-done | bytes 262176 | tf_op jit(solution)/shard_map/ppermute | solution.py:30
  124.5 5.6 %collective-permute-done.22.refs_5_ = bf16[2,128,512]{2,1,0:T(8,128)(2,1)S(1)} collective-permute-done((bf16[2,128,512]{2,1,0:T(8,128)(2,1)S(1)}, bf16[2,128,512]{2,1,0:T(8,128)(2,1)S(1)}, u32[]{:S(2)}, u32[]{:S(2)}) %collective-permute-start.22) | collective-permute-done | bytes 262176 | tf_op jit(solution)/shard_map/ppermute | solution.py:30
  130.1 3.2 %apply_terms.5 = (f32[128,512]{1,0:T(8,128)S(1)}, bf16[128,512]{1,0:T(8,128)(2,1)S(1)}, bf16[128,512]{1,0:T(8,128)(2,1)S(1)}, bf16[128,512]{1,0:T(8,128)(2,1)S(1)}, f32[1,128]{1,0:T(1,128)S(1)}) custom-call(s32[7]{0:T(128)S(1)} %pad_add_fusion.sel, bf16[4,512,512]{2,1,0:T(8,128)(2,1)S(1)} %bitcast.34, bf16[4,512,512]{2,1,0:T(8,128)(2,1)S(1)} %bitcast.37, ...), custom_call_target="tpu_custom_call" | custom-call | tf_op jit(solution)/shard_map/apply_terms/pallas_call | solution.py:85
  134.5 3.2 %collective-permute-start.26 = (bf16[128,512]{1,0:T(8,128)(2,1)S(1)}, bf16[128,512]{1,0:T(8,128)(2,1)S(1)}, u32[]{:S(2)}, u32[]{:S(2)}) collective-permute-start(bf16[128,512]{1,0:T(8,128)(2,1)S(1)} %get-tuple-element.48), channel_id=1, source_target_pairs={{0,1},{1,0},{2,3},{3,2},{4,5},{5,4},{6,7},{7,6},{8,9},{9,8},{10,11... | collective-permute-start | bytes 393224 | tf_op jit(solution)/shard_map/ppermute | solution.py:20
  137.7 9.0 %all_to_all.22.sums = f32[32,1,128]{2,1,0:T(1,128)S(1)} all-to-all(f32[32,1,128]{2,1,0:T(1,128)S(1)} %broadcast_in_dim.60), channel_id=1, replica_groups=mesh['sector'=8,'term'=4] {'sector','term'}, dimensions={0} | all-to-all | bytes 32768 | tf_op jit(solution)/shard_map/all_to_all | solution.py:135
  147.7 9.9 %all_to_all.23 = f32[32,1,128]{2,1,0:T(1,128)S(1)} all-to-all(f32[32,1,128]{2,1,0:T(1,128)S(1)} %broadcast_in_dim.62), channel_id=1, replica_groups=mesh['sector'=8,'term'=4] {'sector','term'}, dimensions={0} | all-to-all | bytes 32768 | tf_op jit(solution)/shard_map/all_to_all | solution.py:135
  (73 shorter events, 31.1 us)
Async XLA Ops:
  1.2 9.6 %collective-permute-start.2 = (bf16[128,512]{1,0:T(8,128)(2,1)S(1)}, bf16[128,512]{1,0:T(8,128)(2,1)S(1)}, u32[]{:S(2)}, u32[]{:S(2)}) collective-permute-start(bf16[128,512]{1,0:T(8,128)(2,1)S(1)} %get-tuple-element.54.refs_0_), channel_id=1, source_target_pairs={{0,3},{1,2},{2,1},{3,0},{4,7},{5,6},{6,5},{7,4},{8,11},{9,10},{10,... | collective-permute-start | bytes 393224 | tf_op jit(solution)/shard_map/ppermute | solution.py:20
  6.4 11.1 %collective-permute-start.1 = (bf16[128,512]{1,0:T(8,128)(2,1)S(1)}, bf16[128,512]{1,0:T(8,128)(2,1)S(1)}, u32[]{:S(2)}, u32[]{:S(2)}) collective-permute-start(bf16[128,512]{1,0:T(8,128)(2,1)S(1)} %get-tuple-element.54.refs_0_), channel_id=1, source_target_pairs={{0,2},{1,3},{2,0},{3,1},{4,6},{5,7},{6,4},{7,5},{8,10},{9,11},{10,... | collective-permute-start | bytes 393224 | tf_op jit(solution)/shard_map/ppermute | solution.py:20
  6.4 11.1 %collective-permute-start = (bf16[128,512]{1,0:T(8,128)(2,1)S(1)}, bf16[128,512]{1,0:T(8,128)(2,1)S(1)}, u32[]{:S(2)}, u32[]{:S(2)}) collective-permute-start(bf16[128,512]{1,0:T(8,128)(2,1)S(1)} %get-tuple-element.54.refs_0_), channel_id=1, source_target_pairs={{0,1},{1,0},{2,3},{3,2},{4,5},{5,4},{6,7},{7,6},{8,9},{9,8},{10,11... | collective-permute-start | bytes 393224 | tf_op jit(solution)/shard_map/ppermute | solution.py:20
  18.3 15.4 %collective-permute-start.3 = (bf16[4,128,512]{2,1,0:T(8,128)(2,1)}, bf16[4,128,512]{2,1,0:T(8,128)(2,1)S(1)}, u32[]{:S(2)}, u32[]{:S(2)}) collective-permute-start(bf16[4,128,512]{2,1,0:T(8,128)(2,1)} %pad_maximum_fusion), channel_id=1, source_target_pairs={{0,4},{4,0},{8,12},{12,8},{16,20},{20,16},{24,28},{28,24},{1,5},{5... | collective-permute-start | bytes 1572872 | tf_op jit(solution)/shard_map/ppermute | solution.py:25
  19.1 9.6 %collective-permute-start.5 = (bf16[2,128,512]{2,1,0:T(8,128)(2,1)}, bf16[2,128,512]{2,1,0:T(8,128)(2,1)S(1)}, u32[]{:S(2)}, u32[]{:S(2)}) collective-permute-start(bf16[2,128,512]{2,1,0:T(8,128)(2,1)} %pad_maximum_fusion.4), channel_id=1, source_target_pairs={{0,28},{4,8},{8,4},{12,16},{16,12},{20,24},{24,20},{28,0},{1,29},{... | collective-permute-start | bytes 786440 | tf_op jit(solution)/shard_map/ppermute | solution.py:30
  22.4 11.4 %collective-permute-start.4 = (bf16[2,128,512]{2,1,0:T(8,128)(2,1)}, bf16[2,128,512]{2,1,0:T(8,128)(2,1)}, u32[]{:S(2)}, u32[]{:S(2)}) collective-permute-start(bf16[2,128,512]{2,1,0:T(8,128)(2,1)} %pad_maximum_fusion.3), channel_id=1, source_target_pairs={{0,28},{4,8},{8,4},{12,16},{16,12},{20,24},{24,20},{28,0},{1,29},{... | collective-permute-start | bytes 786440 | tf_op jit(solution)/shard_map/ppermute | solution.py:30
  39.0 15.7 %collective-permute-start.6 = (bf16[128,512]{1,0:T(8,128)(2,1)S(1)}, bf16[128,512]{1,0:T(8,128)(2,1)S(1)}, u32[]{:S(2)}, u32[]{:S(2)}) collective-permute-start(bf16[128,512]{1,0:T(8,128)(2,1)S(1)} %get-tuple-element.30), channel_id=1, source_target_pairs={{0,3},{1,2},{2,1},{3,0},{4,7},{5,6},{6,5},{7,4},{8,11},{9,10},{10,... | collective-permute-start | bytes 393224 | tf_op jit(solution)/shard_map/ppermute | solution.py:20
  41.5 13.2 %collective-permute-start.7 = (bf16[128,512]{1,0:T(8,128)(2,1)S(1)}, bf16[128,512]{1,0:T(8,128)(2,1)S(1)}, u32[]{:S(2)}, u32[]{:S(2)}) collective-permute-start(bf16[128,512]{1,0:T(8,128)(2,1)S(1)} %get-tuple-element.31), channel_id=1, source_target_pairs={{0,2},{1,3},{2,0},{3,1},{4,6},{5,7},{6,4},{7,5},{8,10},{9,11},{10,... | collective-permute-start | bytes 393224 | tf_op jit(solution)/shard_map/ppermute | solution.py:20
  41.5 13.2 %collective-permute-start.8 = (bf16[128,512]{1,0:T(8,128)(2,1)S(1)}, bf16[128,512]{1,0:T(8,128)(2,1)S(1)}, u32[]{:S(2)}, u32[]{:S(2)}) collective-permute-start(bf16[128,512]{1,0:T(8,128)(2,1)S(1)} %get-tuple-element.32), channel_id=1, source_target_pairs={{0,1},{1,0},{2,3},{3,2},{4,5},{5,4},{6,7},{7,6},{8,9},{9,8},{10,11... | collective-permute-start | bytes 393224 | tf_op jit(solution)/shard_map/ppermute | solution.py:20
  56.6 12.2 %collective-permute-start.10 = (bf16[128,512]{1,0:T(8,128)(2,1)S(1)}, bf16[128,512]{1,0:T(8,128)(2,1)S(1)}, u32[]{:S(2)}, u32[]{:S(2)}) collective-permute-start(bf16[128,512]{1,0:T(8,128)(2,1)S(1)} %get-tuple-element.33.refs_0_), channel_id=1, source_target_pairs={{0,2},{1,3},{2,0},{3,1},{4,6},{5,7},{6,4},{7,5},{8,10},{9,11},{10,... | collective-permute-start | bytes 393224 | tf_op jit(solution)/shard_map/ppermute | solution.py:20
  57.2 11.7 %collective-permute-start.9 = (bf16[128,512]{1,0:T(8,128)(2,1)S(1)}, bf16[128,512]{1,0:T(8,128)(2,1)S(1)}, u32[]{:S(2)}, u32[]{:S(2)}) collective-permute-start(bf16[128,512]{1,0:T(8,128)(2,1)S(1)} %get-tuple-element.33.refs_0_), channel_id=1, source_target_pairs={{0,1},{1,0},{2,3},{3,2},{4,5},{5,4},{6,7},{7,6},{8,9},{9,8},{10,11... | collective-permute-start | bytes 393224 | tf_op jit(solution)/shard_map/ppermute | solution.py:20
  68.9 15.1 %collective-permute-start.12 = (bf16[4,128,512]{2,1,0:T(8,128)(2,1)S(1)}, bf16[4,128,512]{2,1,0:T(8,128)(2,1)S(1)}, u32[]{:S(2)}, u32[]{:S(2)}) collective-permute-start(bf16[4,128,512]{2,1,0:T(8,128)(2,1)S(1)} %pad_maximum_fusion.1), channel_id=1, source_target_pairs={{0,4},{4,0},{8,12},{12,8},{16,20},{20,16},{24,28},{28,24},{1,5},{5... | collective-permute-start | bytes 1572872 | tf_op jit(solution)/shard_map/ppermute | solution.py:25
  69.8 14.3 %collective-permute-start.13 = (bf16[2,128,512]{2,1,0:T(8,128)(2,1)S(1)}, bf16[2,128,512]{2,1,0:T(8,128)(2,1)S(1)}, u32[]{:S(2)}, u32[]{:S(2)}) collective-permute-start(bf16[2,128,512]{2,1,0:T(8,128)(2,1)S(1)} %pad_maximum_fusion.5), channel_id=1, source_target_pairs={{0,28},{4,8},{8,4},{12,16},{16,12},{20,24},{24,20},{28,0},{1,29},{... | collective-permute-start | bytes 786440 | tf_op jit(solution)/shard_map/ppermute | solution.py:30
  87.3 13.3 %collective-permute-start.15 = (bf16[128,512]{1,0:T(8,128)(2,1)S(1)}, bf16[128,512]{1,0:T(8,128)(2,1)S(1)}, u32[]{:S(2)}, u32[]{:S(2)}) collective-permute-start(bf16[128,512]{1,0:T(8,128)(2,1)S(1)} %get-tuple-element.38), channel_id=1, source_target_pairs={{0,3},{1,2},{2,1},{3,0},{4,7},{5,6},{6,5},{7,4},{8,11},{9,10},{10,... | collective-permute-start | bytes 393224 | tf_op jit(solution)/shard_map/ppermute | solution.py:20
  88.7 11.9 %collective-permute-start.16 = (bf16[128,512]{1,0:T(8,128)(2,1)S(1)}, bf16[128,512]{1,0:T(8,128)(2,1)S(1)}, u32[]{:S(2)}, u32[]{:S(2)}) collective-permute-start(bf16[128,512]{1,0:T(8,128)(2,1)S(1)} %get-tuple-element.39), channel_id=1, source_target_pairs={{0,2},{1,3},{2,0},{3,1},{4,6},{5,7},{6,4},{7,5},{8,10},{9,11},{10,... | collective-permute-start | bytes 393224 | tf_op jit(solution)/shard_map/ppermute | solution.py:20
  88.7 11.9 %collective-permute-start.17 = (bf16[128,512]{1,0:T(8,128)(2,1)S(1)}, bf16[128,512]{1,0:T(8,128)(2,1)S(1)}, u32[]{:S(2)}, u32[]{:S(2)}) collective-permute-start(bf16[128,512]{1,0:T(8,128)(2,1)S(1)} %get-tuple-element.40), channel_id=1, source_target_pairs={{0,1},{1,0},{2,3},{3,2},{4,5},{5,4},{6,7},{7,6},{8,9},{9,8},{10,11... | collective-permute-start | bytes 393224 | tf_op jit(solution)/shard_map/ppermute | solution.py:20
  102.1 12.6 %collective-permute-start.19 = (bf16[128,512]{1,0:T(8,128)(2,1)S(1)}, bf16[128,512]{1,0:T(8,128)(2,1)S(1)}, u32[]{:S(2)}, u32[]{:S(2)}) collective-permute-start(bf16[128,512]{1,0:T(8,128)(2,1)S(1)} %get-tuple-element.41.refs_0_), channel_id=1, source_target_pairs={{0,2},{1,3},{2,0},{3,1},{4,6},{5,7},{6,4},{7,5},{8,10},{9,11},{10,... | collective-permute-start | bytes 393224 | tf_op jit(solution)/shard_map/ppermute | solution.py:20
  103.0 11.7 %collective-permute-start.18 = (bf16[128,512]{1,0:T(8,128)(2,1)S(1)}, bf16[128,512]{1,0:T(8,128)(2,1)S(1)}, u32[]{:S(2)}, u32[]{:S(2)}) collective-permute-start(bf16[128,512]{1,0:T(8,128)(2,1)S(1)} %get-tuple-element.41.refs_0_), channel_id=1, source_target_pairs={{0,1},{1,0},{2,3},{3,2},{4,5},{5,4},{6,7},{7,6},{8,9},{9,8},{10,11... | collective-permute-start | bytes 393224 | tf_op jit(solution)/shard_map/ppermute | solution.py:20
  114.8 15.3 %collective-permute-start.21 = (bf16[4,128,512]{2,1,0:T(8,128)(2,1)S(1)}, bf16[4,128,512]{2,1,0:T(8,128)(2,1)S(1)}, u32[]{:S(2)}, u32[]{:S(2)}) collective-permute-start(bf16[4,128,512]{2,1,0:T(8,128)(2,1)S(1)} %pad_maximum_fusion.2), channel_id=1, source_target_pairs={{0,4},{4,0},{8,12},{12,8},{16,20},{20,16},{24,28},{28,24},{1,5},{5... | collective-permute-start | bytes 1572872 | tf_op jit(solution)/shard_map/ppermute | solution.py:25
  114.9 9.6 %collective-permute-start.23 = (bf16[2,128,512]{2,1,0:T(8,128)(2,1)S(1)}, bf16[2,128,512]{2,1,0:T(8,128)(2,1)S(1)}, u32[]{:S(2)}, u32[]{:S(2)}) collective-permute-start(bf16[2,128,512]{2,1,0:T(8,128)(2,1)S(1)} %pad_maximum_fusion.8), channel_id=1, source_target_pairs={{0,28},{4,8},{8,4},{12,16},{16,12},{20,24},{24,20},{28,0},{1,29},{... | collective-permute-start | bytes 786440 | tf_op jit(solution)/shard_map/ppermute | solution.py:30
  116.8 13.3 %collective-permute-start.22 = (bf16[2,128,512]{2,1,0:T(8,128)(2,1)S(1)}, bf16[2,128,512]{2,1,0:T(8,128)(2,1)S(1)}, u32[]{:S(2)}, u32[]{:S(2)}) collective-permute-start(bf16[2,128,512]{2,1,0:T(8,128)(2,1)S(1)} %pad_maximum_fusion.7), channel_id=1, source_target_pairs={{0,28},{4,8},{8,4},{12,16},{16,12},{20,24},{24,20},{28,0},{1,29},{... | collective-permute-start | bytes 786440 | tf_op jit(solution)/shard_map/ppermute | solution.py:30
  133.2 13.5 %collective-permute-start.24 = (bf16[128,512]{1,0:T(8,128)(2,1)S(1)}, bf16[128,512]{1,0:T(8,128)(2,1)S(1)}, u32[]{:S(2)}, u32[]{:S(2)}) collective-permute-start(bf16[128,512]{1,0:T(8,128)(2,1)S(1)} %get-tuple-element.46), channel_id=1, source_target_pairs={{0,3},{1,2},{2,1},{3,0},{4,7},{5,6},{6,5},{7,4},{8,11},{9,10},{10,... | collective-permute-start | bytes 393224 | tf_op jit(solution)/shard_map/ppermute | solution.py:20
  134.5 12.2 %collective-permute-start.25 = (bf16[128,512]{1,0:T(8,128)(2,1)S(1)}, bf16[128,512]{1,0:T(8,128)(2,1)S(1)}, u32[]{:S(2)}, u32[]{:S(2)}) collective-permute-start(bf16[128,512]{1,0:T(8,128)(2,1)S(1)} %get-tuple-element.47), channel_id=1, source_target_pairs={{0,2},{1,3},{2,0},{3,1},{4,6},{5,7},{6,4},{7,5},{8,10},{9,11},{10,... | collective-permute-start | bytes 393224 | tf_op jit(solution)/shard_map/ppermute | solution.py:20
  134.5 12.2 %collective-permute-start.26 = (bf16[128,512]{1,0:T(8,128)(2,1)S(1)}, bf16[128,512]{1,0:T(8,128)(2,1)S(1)}, u32[]{:S(2)}, u32[]{:S(2)}) collective-permute-start(bf16[128,512]{1,0:T(8,128)(2,1)S(1)} %get-tuple-element.48), channel_id=1, source_target_pairs={{0,1},{1,0},{2,3},{3,2},{4,5},{5,4},{6,7},{7,6},{8,9},{9,8},{10,11... | collective-permute-start | bytes 393224 | tf_op jit(solution)/shard_map/ppermute | solution.py:20
  (9 other events, 167.8 us)
